TPU v7x, 128 devices: a whole 4x4x4 slice. The times are simulated.
128 devices in a mesh: tx: 8 (over y, core), ty: 16 (over z, x).
Axes of the slice: x: 4, y: 4, z: 4, core: 2. Of those that a mesh axis runs over, the one named last changes fastest.
Arguments:
- increment: float32 [32, 640, 3072], P(None, 'ty', 'tx'), may hold values from -6 to 6
- vert_rate: float32 [2, 16], replicated, may hold values from 0.05 to 0.8
- zonal_rate: float32 [16, 32], replicated, may hold values from 0.003 to 0.12
- merid_rate: float32 [16, 32], replicated, may hold values from 0.02 to 0.12
- lat_band: int32 [640], replicated, may hold values from 0 to 15, never falling along the last dimension, each value on 1 to 80 neighbouring positions
- slab_owner: int32 [32], replicated, may hold values from 0 to 7, as said below
Outputs:
- covariance_product: float32 [32, 640, 3072], P(None, 'ty', 'tx')
- filtered_slabs: float32 [64, 640, 3072], P('tx', 'ty')
Inputs may be any that keep to these rules, and one draw needn't show every extreme that they name: lat_band never falls along y and every band appears. `slab_owner`: each index of tx owns at most 8 slabs, and some index owns exactly 8.
All inputs are finite; a program needn't handle non-finite values.
Results may differ from a plain program's by a relative error of at most 0.0003.
Values sent between devices are 32-bit elements; how exact they have to be, the bound alone decides.
A program may use at most 128 MiB of HBM per device.

v0:
```python
import jax
import jax.numpy as jnp
from jax import lax
from jax.sharding import PartitionSpec as P

LEV = 16
VAR = 2
NBANDS = 16


HIGHEST_PRECISION = lax.Precision.HIGHEST


def chain_matrices(log_decay, gains):
    length = log_decay.shape[-1]
    inclusive = jnp.cumsum(log_decay, axis=-1)
    exclusive = inclusive - log_decay
    index = jnp.arange(length)
    lower = index[:, None] >= index[None, :]
    upper = index[:, None] <= index[None, :]
    fdiff = inclusive[..., :, None] - inclusive[..., None, :]
    forward = jnp.where(lower, jnp.exp(jnp.where(lower, fdiff, 0.0)), 0.0) * gains[..., None, :]
    bdiff = exclusive[..., None, :] - exclusive[..., :, None]
    backward = jnp.where(upper, jnp.exp(jnp.where(upper, bdiff, 0.0)), 0.0) * gains[..., None, :]
    return (forward, backward)


def gain_of(rates):
    return jnp.sqrt(rates * (2.0 - rates))


def vertical_apply(vert_matrix, values):
    slabs, tile_rows, tile_cols = values.shape
    stacked = values.reshape(VAR, LEV, tile_rows * tile_cols)
    result = jnp.einsum("vlk,vkn->vln", vert_matrix, stacked, precision=HIGHEST_PRECISION)
    return result.reshape(slabs, tile_rows, tile_cols)


def affine_combine(first, second):
    return (first[0] * second[0], second[0] * first[1] + second[1])


def carry_blocks(block_decay, ends):
    scale = jnp.broadcast_to(block_decay, ends.shape)
    inclusive = lax.associative_scan(affine_combine, (scale, ends), axis=2)[1]
    return jnp.concatenate([jnp.zeros_like(inclusive[..., :1]), inclusive[..., :-1]], axis=2)


def carry_row_blocks(block_decay, ends):
    scale = jnp.broadcast_to(block_decay[..., None], ends.shape)
    inclusive = lax.associative_scan(affine_combine, (scale, ends), axis=1)[1]
    return jnp.concatenate([jnp.zeros_like(inclusive[:, :1]), inclusive[:, :-1]], axis=1)


def zonal_filter(values, rates):
    capacity, tile_rows, width = values.shape
    blocks = width // 128
    shaped = values.reshape(capacity, tile_rows, blocks, 128)
    log_decay = jnp.log1p(-rates)[:, :, None, None]
    gains = gain_of(rates)[:, :, None, None]
    offset = jnp.arange(128, dtype=jnp.float32)
    rising = jnp.exp(offset * log_decay)
    falling = jnp.exp(-offset * log_decay)
    index = jnp.arange(128)
    upto = (index[:, None] <= index[None, :]).astype(jnp.float32)
    block_decay = jnp.exp(128.0 * log_decay[..., 0])
    partial_value = jnp.einsum(
        "crbj,ji->crbi", shaped * gains * falling, upto, precision=HIGHEST_PRECISION
    )
    local = rising * partial_value
    entering = carry_blocks(block_decay, local[..., 127])
    forward = local + rising * jnp.exp(log_decay) * entering[..., None]
    partial_back = jnp.einsum(
        "crbj,ij->crbi", forward * gains * rising, upto, precision=HIGHEST_PRECISION
    )
    local_back = falling * partial_back
    from_above = jnp.flip(carry_blocks(block_decay, jnp.flip(local_back[..., 0], 2)), 2)
    backward = local_back + jnp.exp((128.0 - offset) * log_decay) * from_above[..., None]
    return backward.reshape(capacity, tile_rows, width)


def column_filter(values, rates):
    capacity, rows, cols = values.shape
    block = min(rows, 128)
    blocks = rows // block
    shaped = values.reshape(capacity, blocks, block, cols)
    log_decay = jnp.log1p(-rates).reshape(capacity, blocks, block)
    gains = gain_of(rates).reshape(capacity, blocks, block)
    forward_mat, backward_mat = chain_matrices(log_decay, gains)
    local = jnp.einsum("cbij,cbjx->cbix", forward_mat, shaped, precision=HIGHEST_PRECISION)
    inclusive = jnp.cumsum(log_decay, axis=2)
    whole_decay = inclusive[:, :, -1]
    block_decay = jnp.exp(whole_decay)
    entering = carry_row_blocks(block_decay, local[:, :, -1, :])
    forward = local + jnp.exp(inclusive)[..., None] * entering[:, :, None, :]
    local_back = jnp.einsum("cbij,cbjx->cbix", backward_mat, forward, precision=HIGHEST_PRECISION)
    from_above = jnp.flip(
        carry_row_blocks(jnp.flip(block_decay, 1), jnp.flip(local_back[:, :, 0, :], 1)), 1
    )
    exclusive = inclusive - log_decay
    tail = jnp.exp(whole_decay[..., None] - exclusive)
    backward = local_back + tail[..., None] * from_above[:, :, None, :]
    return backward.reshape(capacity, rows, cols)


def shards(increment, vert_rate, zonal_rate, merid_rate, lat_band, slab_owner):
    slabs, tile_rows, tile_cols = increment.shape
    groups_x = lax.axis_size("tx")
    capacity = 2 * slabs // groups_x
    index_x = lax.axis_index("tx")
    index_y = lax.axis_index("ty")
    vert_fwd, vert_bwd = chain_matrices(jnp.log1p(-vert_rate), gain_of(vert_rate))
    vert_matrix = jnp.einsum("vij,vjk->vik", vert_bwd, vert_fwd, precision=HIGHEST_PRECISION)
    vertical = vertical_apply(vert_matrix, increment)
    slab_index = jnp.arange(slabs, dtype=jnp.int32)
    same = slab_owner[:, None] == slab_owner[None, :]
    earlier = slab_index[None, :] < slab_index[:, None]
    slot = jnp.sum(jnp.logical_and(same, earlier), axis=1)
    target = slab_owner * capacity + slot
    slot_rows = jnp.arange(groups_x * capacity, dtype=jnp.int32)
    matches = target[None, :] == slot_rows[:, None]
    source = jnp.sum(jnp.where(matches, slab_index[None, :], 0), axis=1)
    filled = jnp.any(matches, axis=1).astype(jnp.float32)
    outgoing = jnp.take(vertical, source, axis=0) * filled[:, None, None]
    lines = lax.all_to_all(outgoing, "tx", split_axis=0, concat_axis=2, tiled=True)
    mine = lax.dynamic_slice_in_dim(source, index_x * capacity, capacity)
    mine_filled = lax.dynamic_slice_in_dim(filled, index_x * capacity, capacity)
    slab_onehot = (mine[:, None] == slab_index[None, :]).astype(jnp.float32) * mine_filled[:, None]
    band_onehot = (lat_band[:, None] == jnp.arange(NBANDS)[None, :]).astype(jnp.float32)
    row_onehot = lax.dynamic_slice_in_dim(band_onehot, index_y * tile_rows, tile_rows)
    zonal_table = jnp.dot(slab_onehot, zonal_rate.T, precision=HIGHEST_PRECISION)
    merid_table = jnp.dot(slab_onehot, merid_rate.T, precision=HIGHEST_PRECISION)
    zonal_rows = jnp.dot(zonal_table, row_onehot.T, precision=HIGHEST_PRECISION)
    zonal = zonal_filter(lines, zonal_rows)
    columns = lax.all_to_all(zonal, "ty", split_axis=2, concat_axis=1, tiled=True)
    merid_full = jnp.dot(merid_table, band_onehot.T, precision=HIGHEST_PRECISION)
    smoothed_columns = column_filter(columns, merid_full)
    smoothed = lax.all_to_all(smoothed_columns, "ty", split_axis=1, concat_axis=2, tiled=True)
    returned = lax.all_to_all(smoothed, "tx", split_axis=2, concat_axis=0, tiled=True)
    gathered = jnp.take(returned, target, axis=0)
    covariance_product = vertical_apply(vert_matrix, gathered)
    return (covariance_product, smoothed)


def solution(mesh):
    return jax.shard_map(
        shards,
        mesh=mesh,
        in_specs=(P(None, "ty", "tx"), P(), P(), P(), P(), P()),
        out_specs=(P(None, "ty", "tx"), P("tx", "ty", None)),
        check_vma=False,
    )
```

profile of v0, /device:TPU:1, one launch (start us, length us, event | category | flops | bytes accessed | tf_op | source)
XLA Modules:
  0.0 487.3 jit_solution(7366706735983362756)
XLA Ops:
  15.3 6.3 %all-to-all-start = ((f32[64,40,384]{2,1,0:T(8,128)}), f32[64,40,384]{2,1,0:T(8,128)}, u32[]{:S(2)}, u32[]{:S(2)}) async-start(f32[64,40,384]{2,1,0:T(8,128)} %select_multiply_fusion), calls=%async_computation | async-start | bytes 7864320 | tf_op jit(solution)/shard_map/all_to_all | solution.py:125
  22.5 45.0 %all-to-all-done = f32[64,40,384]{2,1,0:T(8,128)} async-done(((f32[64,40,384]{2,1,0:T(8,128)}), f32[64,40,384]{2,1,0:T(8,128)}, u32[]{:S(2)}, u32[]{:S(2)}) %all-to-all-start) | async-done | bytes 3932192 | tf_op jit(solution)/shard_map/all_to_all | solution.py:125
  67.6 6.3 %copy.226 = f32[8,40,8,384]{3,2,1,0:T(8,128)} copy(f32[8,40,8,384]{3,1,0,2:T(8,128)} %bitcast.5) | data formatting | bytes 7864320 | tf_op jit(solution)/shard_map/all_to_all | solution.py:125
  92.1 5.7 %fusion.31 = f32[8,40,24,128]{3,2,1,0:T(8,128)} fusion(f32[8,40,24,128]{3,2,1,0:T(8,128)} %copy-done.2, f32[8,40,24]{2,1,0:T(8,128)S(1)} %concatenate.46.clone, f32[8,40,128]{2,1,0:T(8,128)S(1)} %get-tuple-element.29, f32[8,40]{1,0:T(8,128)S(1)} %get-tuple-element.37, f32[8,40,128]{2,1,0:T(8,128)S(1)} %get-tuple-element.30, ...), kind=kOutput, calls=%fused_computation.34 | convolution fusion | flops 1514881024 | bytes 8387840 | tf_op jit(solution)/shard_map/crbj,ij->crbi/dot_general | solution.py:73
  106.2 7.9 %copy.260 = f32[8,40,24,128]{1,0,3,2:T(8,128)} copy(f32[8,40,24,128]{3,2,1,0:T(8,128)} %multiply_add_fusion.1) | data formatting | bytes 7864320 | tf_op jit(solution)/shard_map/reshape | solution.py:79
  114.1 17.2 %reshape.179 = f32[16,1,61440]{2,1,0:T(1,128)} reshape(f32[3072,8,40]{2,1,0:T(8,128)} %bitcast.74) | data formatting | bytes 7864320
  131.2 8.2 %all-to-all-start.1 = ((f32[16,1,61440]{2,1,0:T(1,128)}), f32[16,1,61440]{2,1,0:T(1,128)}, u32[]{:S(2)}, u32[]{:S(2)}) async-start(f32[16,1,61440]{2,1,0:T(1,128)} %reshape.179), calls=%async_computation.1 | async-start | bytes 7864320 | tf_op jit(solution)/shard_map/all_to_all | solution.py:135
  143.5 53.7 %all-to-all-done.1 = f32[16,1,61440]{2,1,0:T(1,128)} async-done(((f32[16,1,61440]{2,1,0:T(1,128)}), f32[16,1,61440]{2,1,0:T(1,128)}, u32[]{:S(2)}, u32[]{:S(2)}) %all-to-all-start.1) | async-done | bytes 3932192 | tf_op jit(solution)/shard_map/all_to_all | solution.py:135
  197.7 13.6 %reduce.4 = f32[16,61440]{1,0:T(8,128)} reduce(f32[16,1,61440]{2,1,0:T(1,128)} %all-to-all-done.1, f32[]{:T(128)} %broadcast.205), dimensions={1}, to_apply=%all_to_all.51.reduce_sub_computation | reduce | bytes 7864324 | tf_op jit(solution)/shard_map/all_to_all | solution.py:135
  211.4 18.7 %reshape.180 = f32[3072,8,40]{2,1,0:T(8,128)} reshape(f32[16,61440]{1,0:T(8,128)} %reduce.4) | data formatting | bytes 7864320
  230.0 10.9 %copy.236 = f32[8,40,16,192]{3,1,2,0:T(8,128)} copy(f32[8,40,16,192]{1,0,3,2:T(8,128)} %bitcast.75) | data formatting | bytes 7864320 | tf_op jit(solution)/shard_map/all_to_all | solution.py:135
  240.9 11.2 %fusion.11 = f32[8,5,128,192]{2,3,1,0:T(8,128)S(1)} fusion(f32[8,5,128,192]{3,2,1,0:T(8,128)} %bitcast.82, f32[8,5,128]{2,1,0:T(8,128)S(1)} %copy.224, f32[8,5,128]{2,1,0:T(8,128)S(1)} %copy.223, pred[128,128]{1,0:T(8,128)(4,1)S(1)} %iota_compare_fusion.1), kind=kOutput, calls=%fused_computation.16 | convolution fusion | flops 1512570880 | bytes 7921664 | tf_op jit(solution)/shard_map/cbij,cbjx->cbix/dot_general | solution.py:90
  260.8 9.1 %fusion = f32[8,5,128,192]{2,3,1,0:T(8,128)} fusion(f32[8,5,128,192]{2,3,1,0:T(8,128)} %copy-done.3, f32[8,5,192]{2,1,0:T(8,128)S(1)} %concatenate.53.clone, f32[8,5,128]{2,1,0:T(8,128)S(1)} %copy.238, f32[8,5,128]{2,1,0:T(8,128)S(1)} %copy.223, f32[8,5,128]{2,1,0:T(8,128)S(1)} %copy.221, pred[128,128]{1,0:T(8,128)(4,1)S(1)} %iota_compare_fusion.2), kind=kOutput, calls=%fused_computation.3 | convolution fusion | flops 1514536960 | bytes 7972864 | tf_op jit(solution)/shard_map/cbij,cbjx->cbix/dot_general | solution.py:96
  277.9 5.9 %copy.262 = f32[8,5,128,192]{3,0,2,1:T(8,128)} copy(f32[8,5,128,192]{2,3,1,0:T(8,128)} %multiply_add_fusion) | data formatting | bytes 7864320 | tf_op jit(solution)/shard_map/reshape | solution.py:103
  283.8 65.7 %all_to_all.66 = f32[8,640,192]{2,0,1:T(8,128)S(1)} all-to-all(f32[8,640,192]{2,0,1:T(8,128)} %bitcast.80), channel_id=1, replica_groups=mesh['tx'=8,'ty'=16] {'ty'}, dimensions={1} | all-to-all | bytes 7864320 | tf_op jit(solution)/shard_map/all_to_all | solution.py:138
  349.5 5.3 %copy.254 = f32[8,40,16,192]{3,2,1,0:T(8,128)} copy(f32[8,40,16,192]{3,0,1,2:T(8,128)S(1)} %bitcast.81) | data formatting | bytes 7864320 | tf_op jit(solution)/shard_map/all_to_all | solution.py:138
  354.8 5.8 %all_to_all.57 = f32[8,40,3072]{2,1,0:T(8,128)} reshape(f32[8,40,16,192]{3,2,1,0:T(8,128)} %copy.254) | data formatting | bytes 7864320 | tf_op jit(solution)/shard_map/all_to_all | solution.py:138
  360.6 8.8 %copy.255 = f32[8,40,3072]{1,0,2:T(8,128)} copy(f32[8,40,3072]{2,1,0:T(8,128)} %all_to_all.57) | data formatting | bytes 7864320 | tf_op jit(solution)/shard_map/all_to_all | solution.py:138
  369.5 14.8 %reshape.181 = f32[8,1,122880]{2,1,0:T(1,128)} reshape(f32[3072,8,40]{2,1,0:T(8,128)} %bitcast.77) | data formatting | bytes 7864320
  384.3 7.9 %all-to-all-start.3 = ((f32[8,1,122880]{2,1,0:T(1,128)}), f32[8,1,122880]{2,1,0:T(1,128)}, u32[]{:S(2)}, u32[]{:S(2)}) async-start(f32[8,1,122880]{2,1,0:T(1,128)} %reshape.181), calls=%async_computation.3 | async-start | bytes 7864320 | tf_op jit(solution)/shard_map/all_to_all | solution.py:139
  392.2 45.8 %all-to-all-done.3 = f32[8,1,122880]{2,1,0:T(1,128)} async-done(((f32[8,1,122880]{2,1,0:T(1,128)}), f32[8,1,122880]{2,1,0:T(1,128)}, u32[]{:S(2)}, u32[]{:S(2)}) %all-to-all-start.3) | async-done | bytes 3932192 | tf_op jit(solution)/shard_map/all_to_all | solution.py:139
  438.1 13.9 %reduce.5 = f32[8,122880]{1,0:T(8,128)} reduce(f32[8,1,122880]{2,1,0:T(1,128)} %all-to-all-done.3, f32[]{:T(128)} %broadcast.205), dimensions={1}, to_apply=%all_to_all.58.reduce_sub_computation | reduce | bytes 7864324 | tf_op jit(solution)/shard_map/all_to_all | solution.py:139
  452.0 16.8 %reshape.182 = f32[3072,8,40]{2,1,0:T(8,128)} reshape(f32[8,122880]{1,0:T(8,128)} %reduce.5) | data formatting | bytes 7864320
  468.7 9.1 %copy.257 = f32[8,8,40,384]{3,2,1,0:T(8,128)} copy(f32[8,8,40,384]{2,1,3,0:T(8,128)} %bitcast.76) | data formatting | bytes 7864320 | tf_op jit(solution)/shard_map/all_to_all | solution.py:139
  (187 shorter events, 72.1 us)
Async XLA Ops:
  0.6 21.2 %copy-start = (f32[16,32]{1,0:T(8,128)S(1)}, f32[16,32]{1,0:T(8,128)}, u32[]{:S(2)}) copy-start(f32[16,32]{1,0:T(8,128)} %param.8) | copy-start | bytes 6148
  15.3 6.7 %copy-start.4 = (s32[640]{0:T(1024)S(1)}, s32[640]{0:T(1024)}, u32[]{:S(2)}) copy-start(s32[640]{0:T(1024)} %param.10) | copy-start | bytes 7684
  15.3 52.2 %all-to-all-start = ((f32[64,40,384]{2,1,0:T(8,128)}), f32[64,40,384]{2,1,0:T(8,128)}, u32[]{:S(2)}, u32[]{:S(2)}) async-start(f32[64,40,384]{2,1,0:T(8,128)} %select_multiply_fusion), calls=%async_computation | async-start | bytes 7864320 | tf_op jit(solution)/shard_map/all_to_all | solution.py:125
  82.9 1.9 copy-start.2
  131.2 8.2 %copy-start.5 = (f32[16,32]{1,0:T(8,128)S(1)}, f32[16,32]{1,0:T(8,128)}, u32[]{:S(2)}) copy-start(f32[16,32]{1,0:T(8,128)} %param.9) | copy-start | bytes 6148
  131.2 66.0 %all-to-all-start.1 = ((f32[16,1,61440]{2,1,0:T(1,128)}), f32[16,1,61440]{2,1,0:T(1,128)}, u32[]{:S(2)}, u32[]{:S(2)}) async-start(f32[16,1,61440]{2,1,0:T(1,128)} %reshape.179), calls=%async_computation.1 | async-start | bytes 7864320 | tf_op jit(solution)/shard_map/all_to_all | solution.py:135
  252.1 1.9 copy-start.3
  384.3 53.8 %all-to-all-start.3 = ((f32[8,1,122880]{2,1,0:T(1,128)}), f32[8,1,122880]{2,1,0:T(1,128)}, u32[]{:S(2)}, u32[]{:S(2)}) async-start(f32[8,1,122880]{2,1,0:T(1,128)} %reshape.181), calls=%async_computation.3 | async-start | bytes 7864320 | tf_op jit(solution)/shard_map/all_to_all | solution.py:139
  481.9 5.2 %copy-start.1 = (f32[16,32]{1,0:T(8,128)S(1)}, f32[16,32]{1,0:T(8,128)}, u32[]{:S(2)}) copy-start(f32[16,32]{1,0:T(8,128)} %param.8) | copy-start | bytes 6148
where the time goes:
time: 493 us; the launch traced here: 487 us
  local copies, waits for them, and re-layouts  172 us (35%)
  waiting for transfers between devices  145 us (29%)
  blocking collectives  65.7 us (13%)
  other arithmetic  46.2 us (9%)
  matrix products  35 us (7%)
  starting transfers between devices  22.4 us (5%)
    unnamed x24, local copies, waits for them, and re-layouts  73.5 us
    all_to_all x1, blocking collectives, shards(): lax.all_to_all(smoothed_columns, 'ty', split_axis=1, concat_axis=2, tiled...  65.7 us
    all_to_all x1, waiting for transfers between devices, shards(): lax.all_to_all(zonal, 'ty', split_axis=2, concat_axis=1, tiled=True)  53.7 us
    all_to_all x1, waiting for transfers between devices, shards(): lax.all_to_all(smoothed, 'tx', split_axis=2, concat_axis=0, tiled=True)  45.8 us
    all_to_all x1, waiting for transfers between devices, shards(): lax.all_to_all(outgoing, 'tx', split_axis=0, concat_axis=2, tiled=True)  45 us
    all_to_all x3, local copies, waits for them, and re-layouts, shards(): lax.all_to_all(smoothed_columns, 'ty', split_axis=1, concat_axis=2, tiled...  20 us
    all_to_all x1, other arithmetic, shards(): lax.all_to_all(smoothed, 'tx', split_axis=2, concat_axis=0, tiled=True)  13.9 us
    all_to_all x1, other arithmetic, shards(): lax.all_to_all(zonal, 'ty', split_axis=2, concat_axis=1, tiled=True)  13.6 us
  transfers between devices with their start and end apart: 3, of which 3 were waited for; matrix products, arithmetic and copies ran while one was open for 1% of the time, Pallas kernels for 0%

commit v1 on v0

v1 whole, which is shorter than its diff:
```python
import functools

import jax
import jax.numpy as jnp
from jax import lax
from jax.experimental import pallas as pl
from jax.experimental.pallas import tpu as pltpu
from jax.sharding import PartitionSpec as P

MESH = pl.DeviceIdType.MESH
F32 = jnp.float32
BF16 = jnp.bfloat16

LEV = 16
VAR = 2
NB = 16
S = 32
ROWS = 40
W = 384
COLS = 3
NT = 8
NP = 16
CAP = 8
YU = 8


def gain(rate):
    return jnp.sqrt(rate * (2.0 - rate))


def rcopy(src, dst, send, recv, dev):
    return pltpu.make_async_remote_copy(
        src_ref=src, dst_ref=dst, send_sem=send, recv_sem=recv,
        device_id=dev, device_id_type=MESH,
    )


def vertical(buf, vtab):
    def body(i, _):
        v = i // (ROWS // 8)
        rows = pl.ds(pl.multiple_of((i % (ROWS // 8)) * 8, 8), 8)
        base = v * LEV
        state = [jnp.zeros((8, 128), F32)] * COLS
        kept = []
        for l in range(LEV):
            a = vtab[0, base + l]
            g = vtab[1, base + l]
            state = [a * state[c] + g * buf[c, base + l, rows, :] for c in range(COLS)]
            kept.append(state)
        state = [jnp.zeros((8, 128), F32)] * COLS
        for l in reversed(range(LEV)):
            a = vtab[0, base + l]
            g = vtab[1, base + l]
            state = [a * state[c] + g * kept[l][c] for c in range(COLS)]
            for c in range(COLS):
                buf[c, base + l, rows, :] = state[c]
        return 0

    lax.fori_loop(0, VAR * (ROWS // 8), body, 0)


def main_kernel(
    inc, vr, zr, mr, band, owner,
    cov, recv, fbr, mt,
    vbuf, vtab, ldtab, rtab, ftab, matab, mgtab, u1, u2,
    x1h, x1l, x2h, x2l, c1s, c2s, zs, fbuf, albuf, outg, esz, ez,
    es, er, fbsend, fbrecv, fb, bb, fbs, om, otab, mtv,
    src, nxt,
    lsem, s1, r1, s2, r2, s3, r3, s4, r4, s5, r5,
):
    tx = lax.axis_index("tx")
    ty = lax.axis_index("ty")
    bar = pltpu.get_barrier_semaphore()
    for d in range(1, NT):
        pl.semaphore_signal(bar, inc=1, device_id={"tx": lax.rem(tx + d, NT)}, device_id_type=MESH)
    for d in range(1, NP):
        pl.semaphore_signal(bar, inc=1, device_id={"ty": lax.rem(ty + d, NP)}, device_id_type=MESH)
    loads = [
        pltpu.make_async_copy(inc.at[:, :, pl.ds(c * 128, 128)], vbuf.at[c], lsem.at[c])
        for c in range(COLS)
    ]
    for cp in loads:
        cp.start()

    last = [jnp.int32(S)] * NT
    for s in reversed(range(S)):
        own = owner[s]
        nx = jnp.int32(S)
        for o in range(NT):
            hit = own == o
            nx = jnp.where(hit, last[o], nx)
            last[o] = jnp.where(hit, jnp.int32(s), last[o])
        nxt[s] = nx
    nxt[S] = jnp.int32(S)
    for o in range(NT):
        cur = last[o]
        for k in range(CAP):
            src[o * CAP + k] = cur
            cur = nxt[cur]

    for v in range(VAR):
        for l in range(LEV):
            r = jnp.full((8, 128), vr[v, l], F32)
            vtab[0, v * LEV + l] = 1.0 - r
            vtab[1, v * LEV + l] = gain(r)
    eye = lax.broadcasted_iota(jnp.int32, (S, S), 0) == lax.broadcasted_iota(jnp.int32, (S, S), 1)
    lane = lax.broadcasted_iota(jnp.int32, (S, 128), 1)
    lanef = lane.astype(F32)
    sub8 = lax.broadcasted_iota(jnp.int32, (CAP, S), 0)
    slabl = lax.broadcasted_iota(jnp.int32, (CAP, S), 1)
    mine = jnp.full((CAP, S), S, jnp.int32)
    for k in range(CAP):
        mine = jnp.where(sub8 == k, src[tx * CAP + k], mine)
    sel = mine == slabl

    def table(b, _):
        zrow = jnp.broadcast_to(zr[pl.ds(b, 1), :], (S, S))
        zcol = jnp.sum(jnp.where(eye, zrow, 0.0), axis=1, keepdims=True)
        ld = jnp.broadcast_to(jnp.log1p(-zcol), (S, 128))
        ldtab[b] = ld
        for c in range(COLS):
            e = (lanef + float(c * 128)) * ld
            rtab[b, :, c * 128:(c + 1) * 128] = jnp.exp(e)
            ftab[b, :, c * 128:(c + 1) * 128] = jnp.exp(-e)
        mrow = mr[pl.ds(b, 1), :]
        mcol = jnp.sum(jnp.where(eye, jnp.broadcast_to(mrow, (S, S)), 0.0), axis=1, keepdims=True)
        mcol = jnp.broadcast_to(mcol, (S, 128))
        matab[b] = 1.0 - mcol
        mgtab[b] = gain(mcol)
        ocol = jnp.sum(jnp.where(sel, jnp.broadcast_to(mrow, (CAP, S)), 0.0), axis=1, keepdims=True)
        ocol = jnp.broadcast_to(ocol, (CAP, 128))
        otab[0, b] = 1.0 - ocol
        otab[1, b] = gain(ocol)
        return 0

    lax.fori_loop(0, NB, table, 0)

    def tri(i, _):
        rows = pl.ds(pl.multiple_of(i * 16, 16), 16)
        j = lax.broadcasted_iota(jnp.int32, (16, W + 128), 0) + i * 16
        n = lax.broadcasted_iota(jnp.int32, (16, W + 128), 1)
        u1[rows, :] = jnp.where(j <= n, 1.0, 0.0).astype(BF16)
        u2[rows, :] = jnp.where(jnp.logical_or(j > n, n >= W), 1.0, 0.0).astype(BF16)
        return 0

    lax.fori_loop(0, W // 16, tri, 0)
    for c in range(COLS):
        zs[c, S] = jnp.zeros((ROWS, 128), F32)
    fbs[S] = jnp.zeros((8, W), F32)

    for cp in loads:
        cp.wait()
    vertical(vbuf, vtab)
    vflat = vbuf.reshape(COLS, S * ROWS, 128)

    y0 = ty * ROWS

    def pass1(q, _):
        for yy in range(YU):
            y = q * YU + yy
            b = band[y0 + y]
            rows = slice(yy * S, (yy + 1) * S)
            for c in range(COLS):
                ls = slice(c * 128, (c + 1) * 128)
                u = vflat[c, pl.ds(y, S, stride=ROWS), :]
                x1 = u * ftab[b, :, ls]
                x2 = u * rtab[b, :, ls]
                h1 = x1.astype(BF16)
                h2 = x2.astype(BF16)
                x1h[rows, ls] = h1
                x2h[rows, ls] = h2
                x1l[rows, ls] = (x1 - h1.astype(F32)).astype(BF16)
                x2l[rows, ls] = (x2 - h2.astype(F32)).astype(BF16)
        rows = pl.ds(pl.multiple_of(q * (YU * S), YU * S), YU * S)
        c1s[rows, :] = jnp.dot(x1h[...], u1[...], preferred_element_type=F32) + jnp.dot(
            x1l[...], u1[...], preferred_element_type=F32)
        c2s[rows, :] = jnp.dot(x2h[...], u2[...], preferred_element_type=F32) + jnp.dot(
            x2l[...], u2[...], preferred_element_type=F32)
        return 0

    lax.fori_loop(0, ROWS // YU, pass1, 0)

    def pack(y, carry):
        e, s, ld = carry
        rows = pl.ds(pl.multiple_of(y * S, S), S)
        here = lane == y
        e = jnp.where(here, c1s[rows, W:W + 128], e)
        s = jnp.where(here, c2s[rows, W:W + 128], s)
        ld = jnp.where(here, ldtab[band[y0 + y]], ld)
        return e, s, ld

    zero = jnp.zeros((S, 128), F32)
    e, s, ld = lax.fori_loop(0, ROWS, pack, (zero, zero, zero))
    esz[0] = e * jnp.exp(float(W - 1) * ld)
    esz[1] = s
    aw = jnp.exp(float(W) * ld)
    a1 = jnp.exp(ld)

    pl.semaphore_wait(bar, NT + NP - 2)

    def x1(d, here):
        p = lax.rem(tx + d, NT)
        q = p if here else tx
        return rcopy(esz, ez.at[q], s1.at[d], r1.at[q], {"tx": p})

    for d in range(1, NT):
        x1(d, False).start()
    ez[tx] = esz[...]
    for d in range(1, NT):
        x1(d, True).wait_recv()
    rin = zero
    rmine = zero
    for t in range(NT):
        rmine = jnp.where(tx == t, rin, rmine)
        rin = ez[t, 0] + aw * rin
    tin = -a1 * rin
    tmine = zero
    for t in reversed(range(NT)):
        tmine = jnp.where(tx == t, tin, tmine)
        tin = ez[t, 1] + aw * tin
    pp = a1 * rmine
    qq = aw * tmine

    zflat = zs.reshape(COLS, (S + 1) * ROWS, 128)

    zcar = tuple(jnp.zeros((S, 128), F32) for _ in range(COLS))

    def pass2(q, carry):
        state, al = list(carry[0]), carry[1]
        for yy in range(YU):
            y = q * YU + yy
            b = band[y0 + y]
            p = jnp.sum(jnp.where(lane == y, pp, 0.0), axis=1, keepdims=True)
            qv = jnp.sum(jnp.where(lane == y, qq, 0.0), axis=1, keepdims=True)
            rows = pl.ds(pl.multiple_of(y * S, S), S)
            a = matab[b]
            g = mgtab[b]
            for c in range(COLS):
                ls = slice(c * 128, (c + 1) * 128)
                z = rtab[b, :, ls] * (c1s[rows, ls] + p) + ftab[b, :, ls] * (c2s[rows, ls] + qv)
                zflat[c, pl.ds(y, S, stride=ROWS), :] = z
                state[c] = a * state[c] + g * z
                fbuf[rows, ls] = state[c]
            al = a * al
            albuf[rows, :] = al
        return tuple(state), al

    state, al = lax.fori_loop(0, ROWS // YU, pass2, (zcar, jnp.ones((S, 128), F32)))

    def x2(d, here):
        p = lax.rem(tx + d, NT)
        q = p if here else tx
        return rcopy(outg.at[p], recv.at[q], s2.at[d], r2.at[q], {"tx": p})

    for d in (4, 5, 3, 2, 6, 7, 1, 0):
        p = lax.rem(tx + d, NT)

        def fill(k, _):
            slab = src[p * CAP + k]
            for c in range(COLS):
                outg[p, c, pl.ds(pl.multiple_of(k * ROWS, 8), ROWS), :] = zs[c, slab]
            return 0

        lax.fori_loop(0, CAP, fill, 0)
        if d:
            x2(d, False).start()
        else:
            own_copy = pltpu.make_async_copy(outg.at[tx], recv.at[tx], lsem.at[0])
            own_copy.start()

    def back(i, carry):
        st, gm = list(carry[0]), carry[1]
        for k in range(4):
            y = ROWS - 1 - (i * 4 + k)
            b = band[y0 + y]
            rows = pl.ds(pl.multiple_of(y * S, S), S)
            a = matab[b]
            g = mgtab[b]
            for c in range(COLS):
                st[c] = a * st[c] + g * fbuf[rows, c * 128:(c + 1) * 128]
            gm = a * gm + g * albuf[rows, :]
        return tuple(st), gm

    first, gm = lax.fori_loop(0, ROWS // 4, back, (zcar, zero))
    for t in range(NP):
        two = slice(2 * t, 2 * t + 2)
        for c in range(COLS):
            ls = slice(c * 128, (c + 1) * 128)
            es[t, 0:2, ls] = state[c][two]
            es[t, 2:4, ls] = first[c][two]
            es[t, 4:6, ls] = al[two]
            es[t, 6:8, ls] = gm[two]

    def x3(d, here):
        p = lax.rem(ty + d, NP)
        q = p if here else ty
        return rcopy(es.at[p], er.at[q], s3.at[d], r3.at[q], {"ty": p})

    for d in range(1, NP):
        x3(d, False).start()
    er[ty] = es[ty]
    for d in range(1, NP):
        x3(d, True).wait_recv()
    f = jnp.zeros((2, W), F32)
    for p in range(NP):
        fbsend[p, 0:2, :] = f
        f = er[p, 0:2, :] + er[p, 4:6, :] * f
    bk = jnp.zeros((2, W), F32)
    for p in reversed(range(NP)):
        fbsend[p, 2:4, :] = bk
        fbsend[p, 4:8, :] = jnp.zeros((4, W), F32)
        bk = er[p, 2:4, :] + er[p, 6:8, :] * fbsend[p, 0:2, :] + er[p, 4:6, :] * bk

    def x4(d, here):
        p = lax.rem(ty + d, NP)
        q = p if here else ty
        return rcopy(fbsend.at[p], fbrecv.at[q], s4.at[d], r4.at[q], {"ty": p})

    for d in range(1, NP):
        x4(d, False).start()
    fbrecv[ty] = fbsend[ty]
    for d in range(1, NP):
        x4(d, True).wait_recv()
    for t in range(NP):
        fb[2 * t:2 * t + 2, :] = fbrecv[t, 0:2, :]
        bb[2 * t:2 * t + 2, :] = fbrecv[t, 2:4, :]
        for j in range(2):
            fbs[2 * t + j, 0:1, :] = fbrecv[t, j:j + 1, :]
            fbs[2 * t + j, 1:2, :] = fbrecv[t, 2 + j:3 + j, :]
    for o in range(NT):
        for k in range(CAP):
            slab = src[o * CAP + k]
            om[o, 0, k:k + 1, :] = fbs[slab, 0:1, :]
            om[o, 1, k:k + 1, :] = fbs[slab, 1:2, :]

    def x5(d, here):
        p = lax.rem(tx + d, NT)
        q = p if here else tx
        return rcopy(om.at[p], fbr.at[q], s5.at[d], r5.at[q], {"tx": p})

    for d in range(1, NT):
        x5(d, False).start()
    own_fb = pltpu.make_async_copy(om.at[tx], fbr.at[tx], lsem.at[1])
    own_fb.start()

    def rates(y, _):
        b = band[y0 + y]
        mtv[0, y] = otab[0, b]
        mtv[1, y] = otab[1, b]
        return 0

    lax.fori_loop(0, ROWS, rates, 0)
    mt_copy = pltpu.make_async_copy(mtv, mt, lsem.at[2])
    mt_copy.start()

    fin = [fb[:, c * 128:(c + 1) * 128] for c in range(COLS)]

    def smooth(i, st):
        st = list(st)
        for k in range(4):
            y = ROWS - 1 - (i * 4 + k)
            b = band[y0 + y]
            rows = pl.ds(pl.multiple_of(y * S, S), S)
            a = matab[b]
            g = mgtab[b]
            alp = albuf[rows, :]
            for c in range(COLS):
                st[c] = a * st[c] + g * (fbuf[rows, c * 128:(c + 1) * 128] + alp * fin[c])
                vflat[c, pl.ds(y, S, stride=ROWS), :] = st[c]
        return tuple(st)

    lax.fori_loop(0, ROWS // 4, smooth, tuple(bb[:, c * 128:(c + 1) * 128] for c in range(COLS)))
    vertical(vbuf, vtab)
    stores = [
        pltpu.make_async_copy(vbuf.at[c], cov.at[:, :, pl.ds(c * 128, 128)], lsem.at[3 + c])
        for c in range(COLS)
    ]
    for cp in stores:
        cp.start()
    for cp in stores:
        cp.wait()
    own_copy.wait()
    own_fb.wait()
    mt_copy.wait()
    for d in range(1, NT):
        x1(d, False).wait_send()
        x2(d, False).wait_send()
        x2(d, True).wait_recv()
        x5(d, False).wait_send()
        x5(d, True).wait_recv()
    for d in range(1, NP):
        x3(d, False).wait_send()
        x4(d, False).wait_send()


def final_kernel(recv, fbr, mt, out, tmp):
    def col(c, _):
        kept = []
        f = fbr[0, 0, c]
        for y in range(ROWS):
            f = mt[0, y] * f + mt[1, y] * recv[0, c, pl.ds(y, CAP, stride=ROWS), :]
            kept.append(f)
        b = fbr[0, 1, c]
        for y in reversed(range(ROWS)):
            b = mt[0, y] * b + mt[1, y] * kept[y]
            tmp[c, pl.ds(y, CAP, stride=ROWS), :] = b
        return 0

    lax.fori_loop(0, COLS, col, 0)
    for c in range(COLS):
        for k in range(CAP):
            out[k, :, c * 128:(c + 1) * 128] = tmp[c, k * ROWS:(k + 1) * ROWS, :]


def shards(increment, vert_rate, zonal_rate, merid_rate, lat_band, slab_owner):
    vm = pltpu.VMEM
    dma = pltpu.SemaphoreType.DMA
    anyspace = pl.BlockSpec(memory_space=pl.ANY)
    vspec = pl.BlockSpec(memory_space=pltpu.VMEM)
    sspec = pl.BlockSpec(memory_space=pltpu.SMEM)
    cov, recv, fbr, mt = pl.pallas_call(
        main_kernel,
        out_shape=(
            jax.ShapeDtypeStruct((S, ROWS, W), F32),
            jax.ShapeDtypeStruct((NT, COLS, CAP * ROWS, 128), F32),
            jax.ShapeDtypeStruct((NT, 2, CAP, W), F32),
            jax.ShapeDtypeStruct((2, ROWS, CAP, 128), F32),
        ),
        in_specs=[anyspace, sspec, vspec, vspec, sspec, sspec],
        out_specs=(anyspace, anyspace, anyspace, anyspace),
        scratch_shapes=[
            vm((COLS, S, ROWS, 128), F32),
            vm((2, VAR * LEV, 8, 128), F32),
            vm((NB, S, 128), F32),
            vm((NB, S, W), F32),
            vm((NB, S, W), F32),
            vm((NB, S, 128), F32),
            vm((NB, S, 128), F32),
            vm((W, W + 128), BF16),
            vm((W, W + 128), BF16),
            vm((YU * S, W), BF16),
            vm((YU * S, W), BF16),
            vm((YU * S, W), BF16),
            vm((YU * S, W), BF16),
            vm((ROWS * S, W + 128), F32),
            vm((ROWS * S, W + 128), F32),
            vm((COLS, S + 1, ROWS, 128), F32),
            vm((ROWS * S, W), F32),
            vm((ROWS * S, 128), F32),
            vm((NT, COLS, CAP * ROWS, 128), F32),
            vm((2, S, 128), F32),
            vm((NT, 2, S, 128), F32),
            vm((NP, 8, W), F32),
            vm((NP, 8, W), F32),
            vm((NP, 8, W), F32),
            vm((NP, 8, W), F32),
            vm((S, W), F32),
            vm((S, W), F32),
            vm((S + 1, 8, W), F32),
            vm((NT, 2, CAP, W), F32),
            vm((2, NB, CAP, 128), F32),
            vm((2, ROWS, CAP, 128), F32),
            pltpu.SMEM((NT * CAP,), jnp.int32),
            pltpu.SMEM((S + 1,), jnp.int32),
            dma((6,)),
            dma((NT,)), dma((NT,)),
            dma((NT,)), dma((NT,)),
            dma((NP,)), dma((NP,)),
            dma((NP,)), dma((NP,)),
            dma((NT,)), dma((NT,)),
        ],
        compiler_params=pltpu.CompilerParams(
            collective_id=0, has_side_effects=True, vmem_limit_bytes=56 * 1024 * 1024
        ),
        name="filter_exchange",
    )(increment, vert_rate, zonal_rate, merid_rate, lat_band, slab_owner)
    fbr = fbr.reshape(NT, 2, CAP, COLS, 128).transpose(0, 1, 3, 2, 4)
    filtered = pl.pallas_call(
        final_kernel,
        grid=(NT,),
        out_shape=jax.ShapeDtypeStruct((CAP, ROWS, NT * W), F32),
        in_specs=[
            pl.BlockSpec((1, COLS, CAP * ROWS, 128), lambda t: (t, 0, 0, 0)),
            pl.BlockSpec((1, 2, COLS, CAP, 128), lambda t: (t, 0, 0, 0, 0)),
            pl.BlockSpec((2, ROWS, CAP, 128), lambda t: (0, 0, 0, 0)),
        ],
        out_specs=pl.BlockSpec((CAP, ROWS, W), lambda t: (0, 0, t)),
        scratch_shapes=[vm((COLS, CAP * ROWS, 128), F32)],
        name="owner_columns",
    )(recv, fbr, mt)
    return cov, filtered


def solution(mesh):
    return jax.shard_map(
        shards,
        mesh=mesh,
        in_specs=(P(None, "ty", "tx"), P(), P(), P(), P(), P()),
        out_specs=(P(None, "ty", "tx"), P("tx", "ty", None)),
        check_vma=False,
    )
```

time: 493 us -> 75.8 us (0.15); the launches traced: 487 us -> 75.5 us
  local copies, waits for them, and re-layouts: 172 us -> 1.28 us
  waiting for transfers between devices: 145 us -> 0 us
  Pallas kernels: 0 us -> 73.5 us
  blocking collectives: 65.7 us -> 0 us
  other arithmetic: 46.2 us -> 0 us
  matrix products: 35 us -> 0 us
  starting transfers between devices: 22.4 us -> 0 us
    all_to_all x3 -> x0, waiting for transfers between devices: 145 us -> none  [the longest x1 53.7 us: shards(): lax.all_to_all(zonal, 'ty', split_axis=2, concat_axis=1, tiled=True)]
    pallas_call x0 -> x2, Pallas kernels: none -> 73.5 us  [the longest x1 64.9 us: shards(): pl.pallas_call(main_kernel, out_shape=(jax.ShapeDtypeStruct((S, ROWS, W),...]
    unnamed x24 -> x3, local copies, waits for them, and re-layouts: 73.5 us -> 1.28 us
    all_to_all x1 -> x0, blocking collectives: 65.7 us -> none  [shards(): lax.all_to_all(smoothed_columns, 'ty', split_axis=1, concat_axis=2, tiled...]
    all_to_all x7 -> x0, local copies, waits for them, and re-layouts: 46.8 us -> none  [the longest x3 20 us: shards(): lax.all_to_all(smoothed_columns, 'ty', split_axis=1, concat_axis=2, tiled...]
    dot_general x11 -> x0, matrix products: 35 us -> none  [the longest x1 11.2 us: column_filter(): jnp.einsum('cbij,cbjx->cbix', forward_mat, shaped, precision=HIGHEST_PREC...]
    all_to_all x2 -> x0, other arithmetic: 27.5 us -> none  [the longest x1 13.9 us: shards(): lax.all_to_all(smoothed, 'tx', split_axis=2, concat_axis=0, tiled=True)]
    all_to_all x3 -> x0, starting transfers between devices: 22.4 us -> none  [the longest x1 8.19 us: shards(): lax.all_to_all(zonal, 'ty', split_axis=2, concat_axis=1, tiled=True)]
  transfers between devices with their start and end apart: 3 -> 0, of which waited for: 3 -> 0; matrix products, arithmetic and copies ran while one was open for 1% -> 0% of each run, Pallas kernels for 0% -> 0%
where the time goes in v1:
time: 75.8 us; the launch traced here: 75.5 us
  Pallas kernels  73.5 us (97%)
  local copies, waits for them, and re-layouts  1.28 us (2%)
    pallas_call x1, Pallas kernels, shards(): pl.pallas_call(main_kernel, out_shape=(jax.ShapeDtypeStruct((S, ROWS, W),...  64.9 us
    pallas_call x1, Pallas kernels, shards(): pl.pallas_call(final_kernel, grid=(NT,), out_shape=jax.ShapeDtypeStruct((...  8.63 us

profile of v1, /device:TPU:1, one launch (start us, length us, event | category | flops | bytes accessed | tf_op | source)
XLA Modules:
  0.0 75.5 jit_solution(14498694786396562705)
XLA Ops:
  0.6 64.9 %filter_exchange.1 = (f32[32,40,384]{2,1,0:T(8,128)}, f32[8,3,320,128]{3,2,1,0:T(8,128)}, f32[8,2,8,384]{3,2,1,0:T(8,128)}, f32[2,40,8,128]{3,2,1,0:T(8,128)}) custom-call(f32[32,40,384]{2,1,0:T(8,128)} %inc.1, f32[2,16]{1,0:T(2,128)} %vr.1, f32[16,32]{1,0:T(8,128)} %zr.1, f32[16,32]{1,0:T(8,128)} %mr.1, s32[640]{0:T(1024)} %band.1, s32[32]{0:T(128)} %owner.1), custom_call_target="tpu_custom_call" | custom-call | tf_op jit(solution)/shard_map/filter_exchange/pallas_call | solution.py:421
  65.6 0.0 copy-start
  65.6 8.6 %owner_columns.1 = f32[8,40,3072]{2,1,0:T(8,128)} custom-call(f32[8,3,320,128]{3,2,1,0:T(8,128)} %get-tuple-element.7.recv, f32[8,2,3,8,128]{4,3,2,1,0:T(8,128)} %bitcast.3, f32[2,40,8,128]{3,2,1,0:T(8,128)} %get-tuple-element.9.mt), custom_call_target="tpu_custom_call" | custom-call | tf_op jit(solution)/shard_map/owner_columns/pallas_call | solution.py:478
  74.2 0.0 copy-done
  74.2 1.3 %copy.9 = f32[32,40,384]{2,1,0:T(8,128)} copy(f32[32,40,384]{2,1,0:T(8,128)S(1)} %copy-done) | data formatting | bytes 3932160
Async XLA Ops:
  65.6 8.6 %copy-start = (f32[32,40,384]{2,1,0:T(8,128)S(1)}, f32[32,40,384]{2,1,0:T(8,128)}, u32[]{:S(2)}) copy-start(f32[32,40,384]{2,1,0:T(8,128)} %get-tuple-element.12) | copy-start | bytes 5898244
